TPU v7x, 32 devices: a whole 2x2x4 slice. The times are simulated.
32 devices in a mesh: pages: 2 (over y), tile: 4 (over z), mp: 2 (over x), batch: 2 (over core).
Axes of the slice: x: 2, y: 2, z: 4, core: 2. Of those that a mesh axis runs over, the one named last changes fastest.
Arguments:
- page_cells: bfloat16 [4, 48, 24, 1024], P(('pages', 'batch'), 'tile'), parts along dimension 0, may hold values from -40 to 40
- text_states: bfloat16 [4, 1024, 1024], P(('pages', 'batch'), 'tile'), parts along dimension 0, may hold values from -40 to 40
- enc_query: bfloat16 [1024, 1024], P('batch', 'mp'), may hold values from -2.5 to 2.5
- enc_keyval: bfloat16 [1024, 2, 1024], P('batch', None, 'mp'), may hold values from -0.1875 to 0.1875
- enc_proj: bfloat16 [1024, 1024], P('mp', 'batch'), may hold values from -0.1875 to 0.1875
- dec_query: bfloat16 [1024, 1024], P('batch', 'mp'), may hold values from -2.5 to 2.5
- dec_keyval: bfloat16 [1024, 2, 1024], P('batch', None, 'mp'), may hold values from -0.1875 to 0.1875
- dec_out: bfloat16 [1024, 1024], P('mp', 'batch'), may hold values from -0.1875 to 0.1875
Outputs:
- encoded: bfloat16 [4, 48, 24, 1024], P(('pages', 'batch'), 'tile'), parts along dimension 0
- decoded: bfloat16 [4, 1024, 1024], P(('pages', 'batch'), ('tile', 'mp')), parts along dimension 0
There are 2 independent parts, one for each index of `pages`. A program takes and returns all parts, laid end to end along the dimension named above; an argument that names none is the same for every part. Nothing has to cross between parts.
All inputs are finite; a program needn't handle non-finite values.
Results may differ from a plain program's by a relative error of at most 0.012.
Values may be sent and summed in bfloat16 or wider, within the bound.
No kernel may reach another device: no remote copies, remote signals or barrier semaphores. Data moves between devices by JAX's collectives and lax.ppermute only.
A program may use at most 64 MiB of HBM per device.

v0:
```python
import math
import jax
import jax.numpy as jnp
from jax import lax
from jax.sharding import PartitionSpec as P

HEAD_ENC = 32
HEAD_DEC = 64


def from_behind(value, axis, by):
    devices = lax.axis_size(axis)
    return lax.ppermute(value, axis, [(i, (i + by) % devices) for i in range(devices)])


def layer_norm(values):
    center = values - jnp.mean(values, axis=-1, keepdims=True)
    variance = jnp.mean(center * center, axis=-1, keepdims=True)
    return center / jnp.sqrt(variance + 1e-05)


def regions(length, window, offset):
    index_row = jnp.arange(length, dtype=jnp.int32)
    return jnp.where(
        index_row < length - window, 0, jnp.where(index_row < length - offset, 1, 2)
    ).astype(jnp.int32)


def body(page_cells, text_states, enc_query, enc_keyval, enc_proj, dec_query, dec_keyval, dec_out):
    wq_enc, wkv_enc, wproj_enc, wq_dec, wkv_dec, wout_dec = (
        lax.all_gather(enc_query, "batch", axis=0, tiled=True),
        lax.all_gather(enc_keyval, "batch", axis=0, tiled=True),
        lax.all_gather(enc_proj, "batch", axis=1, tiled=True),
        lax.all_gather(dec_query, "batch", axis=0, tiled=True),
        lax.all_gather(dec_keyval, "batch", axis=0, tiled=True),
        lax.all_gather(dec_out, "batch", axis=1, tiled=True),
    )
    pages_here, window, columns, width = page_cells.shape
    offset = window // 2
    own_rows = window * columns
    hq_enc = wq_enc.shape[1]
    heads_enc = hq_enc // HEAD_ENC
    joined = jnp.concatenate([wq_enc, wkv_enc.reshape(width, 2 * hq_enc)], axis=1)
    rows_below = from_behind(page_cells[:, :offset], "tile", -1)
    normed = layer_norm(
        jnp.concatenate([page_cells[:, offset:], rows_below], axis=1).astype(jnp.float32)
    ).astype(jnp.bfloat16)
    projected = jnp.einsum(
        "prcd,de->prce", normed, joined, preferred_element_type=jnp.float32
    ).astype(jnp.bfloat16)
    projected = jnp.roll(projected, -offset, axis=2)
    per_row = columns // window
    shaped = projected.reshape(pages_here, window, per_row, window, 3, heads_enc, HEAD_ENC)
    shaped = jnp.swapaxes(shaped, 1, 2).reshape(
        pages_here, per_row, window * window, 3, heads_enc, HEAD_ENC
    )
    win_q = shaped[:, :, :, 0]
    win_k = shaped[:, :, :, 1]
    win_v = shaped[:, :, :, 2]
    is_last = lax.axis_index("tile") == lax.axis_size("tile") - 1
    local_rows = jnp.arange(window, dtype=jnp.int32)
    row_region = jnp.where(is_last, jnp.where(local_rows < window - offset, 1, 2), 0).astype(
        jnp.int32
    )
    labels = row_region[:, None] * 3 + regions(columns, window, offset)[None, :]
    labels = jnp.swapaxes(labels.reshape(window, per_row, window), 0, 1).reshape(
        per_row, window * window
    )
    allowed = labels[:, :, None] == labels[:, None, :]
    win_scores = jnp.einsum(
        "pnqhd,pnkhd->pnhqk", win_q, win_k, preferred_element_type=jnp.float32
    ) / math.sqrt(HEAD_ENC)
    win_scores = jnp.where(allowed[None, :, None], win_scores, -jnp.inf)
    top = jnp.max(win_scores, axis=-1, keepdims=True)
    expd = jnp.exp(win_scores - top)
    win_weights = (expd / jnp.sum(expd, axis=-1, keepdims=True)).astype(jnp.bfloat16)
    win_out = jnp.einsum(
        "pnhqk,pnkhd->pnqhd", win_weights, win_v, preferred_element_type=jnp.float32
    ).astype(jnp.bfloat16)
    win_out = win_out.reshape(pages_here, per_row, window, window, hq_enc)
    win_out = jnp.swapaxes(win_out, 1, 2).reshape(pages_here, window, columns, hq_enc)
    win_out = jnp.roll(win_out, offset, axis=2)
    rows_above = from_behind(win_out[:, window - offset :], "tile", 1)
    unrolled = jnp.concatenate([rows_above, win_out[:, : window - offset]], axis=1)
    partial_proj = jnp.einsum(
        "prce,ed->prcd", unrolled, wproj_enc, preferred_element_type=jnp.float32
    )
    summed = lax.psum(partial_proj.astype(jnp.bfloat16), "mp").astype(jnp.float32)
    encoded = (page_cells.astype(jnp.float32) + summed).astype(jnp.bfloat16)
    hq_dec = wq_dec.shape[1]
    heads_dec = hq_dec // HEAD_DEC
    page_normed = (
        layer_norm(encoded.astype(jnp.float32))
        .astype(jnp.bfloat16)
        .reshape(pages_here, own_rows, width)
    )
    page_kv = jnp.einsum(
        "pnd,de->pne",
        page_normed,
        wkv_dec.reshape(width, 2 * hq_dec),
        preferred_element_type=jnp.float32,
    ).astype(jnp.bfloat16)
    text_normed = layer_norm(text_states.astype(jnp.float32)).astype(jnp.bfloat16)
    queries = jnp.einsum(
        "ptd,de->pte", text_normed, wq_dec, preferred_element_type=jnp.float32
    ).astype(jnp.bfloat16)
    text_len = text_states.shape[1]
    query_heads = queries.reshape(pages_here, text_len, heads_dec, HEAD_DEC)
    start_state = (
        jnp.full((pages_here, heads_dec, text_len), -jnp.inf, jnp.float32),
        jnp.zeros((pages_here, heads_dec, text_len), jnp.float32),
        jnp.zeros((pages_here, heads_dec, text_len, HEAD_DEC), jnp.float32),
    )
    carried = start_state
    shard_rows = lax.all_gather(page_kv, "tile", axis=1, tiled=True)
    count = shard_rows.shape[1] // own_rows
    grouped = max(
        (
            factor
            for factor in range(1, count + 1)
            if count % factor == 0 and factor * own_rows <= 2048
        )
    )
    blocks = jnp.moveaxis(
        shard_rows.reshape(pages_here, count // grouped, grouped * own_rows, 2 * hq_dec), 1, 0
    )

    def advance(running, block_kv):
        maxima, totals, accum = running
        span = block_kv.shape[1]
        block_keys = block_kv[..., :hq_dec].reshape(pages_here, span, heads_dec, HEAD_DEC)
        block_vals = block_kv[..., hq_dec:].reshape(pages_here, span, heads_dec, HEAD_DEC)
        cross_scores = jnp.einsum(
            "pqhd,pkhd->phqk", query_heads, block_keys, preferred_element_type=jnp.float32
        ) / math.sqrt(HEAD_DEC)
        newest = jnp.maximum(maxima, jnp.max(cross_scores, axis=-1))
        rescale = jnp.exp(maxima - newest)
        expo = jnp.exp(cross_scores - newest[..., None])
        totals = totals * rescale + jnp.sum(expo, axis=-1)
        accum = accum * rescale[..., None] + jnp.einsum(
            "phqk,pkhd->phqd",
            expo.astype(jnp.bfloat16),
            block_vals,
            preferred_element_type=jnp.float32,
        )
        return ((newest, totals, accum), None)

    carried, unused = lax.scan(advance, carried, blocks)
    maxima, totals, accum = carried
    context = (
        jnp.transpose(accum / totals[..., None], (0, 2, 1, 3))
        .reshape(pages_here, text_len, hq_dec)
        .astype(jnp.bfloat16)
    )
    share = text_len // lax.axis_size("mp")
    mixed = lax.psum_scatter(
        jnp.einsum("pte,ed->tpd", context, wout_dec, preferred_element_type=jnp.float32).astype(
            jnp.bfloat16
        ),
        "mp",
        scatter_dimension=0,
        tiled=True,
    ).astype(jnp.float32)
    own_text = lax.dynamic_slice_in_dim(text_states, lax.axis_index("mp") * share, share, 1)
    decoded = (own_text.astype(jnp.float32) + jnp.moveaxis(mixed, 0, 1)).astype(jnp.bfloat16)
    return (encoded, decoded)


def solution(mesh):
    placed = (
        P(("pages", "batch"), "tile", None, None),
        P(("pages", "batch"), "tile", None),
        P("batch", "mp"),
        P("batch", None, "mp"),
        P("mp", "batch"),
        P("batch", "mp"),
        P("batch", None, "mp"),
        P("mp", "batch"),
    )
    return jax.shard_map(
        body,
        mesh=mesh,
        in_specs=placed,
        out_specs=(
            P(("pages", "batch"), "tile", None, None),
            P(("pages", "batch"), ("tile", "mp"), None),
        ),
        check_vma=False,
    )
```

profile of v0, /device:TPU:0, one launch (start us, length us, event | category | flops | bytes accessed | tf_op | source)
XLA Modules:
  0.0 199.5 jit_solution(16749749369688853707)
XLA Ops:
  9.6 5.1 %collective-permute-start = (bf16[1,6,24,1024]{3,2,1,0:T(8,128)(2,1)S(1)}, bf16[1,6,24,1024]{3,2,1,0:T(8,128)(2,1)S(1)}, u32[]{:S(2)}, u32[]{:S(2)}) collective-permute-start(bf16[1,6,24,1024]{3,2,1,0:T(8,128)(2,1)S(1)} %get-tuple-element.29), channel_id=1, source_target_pairs={{0,12},{4,0},{8,4},{12,8},{1,13},{5,1},{9,5},{13,9},{2,14},{6,2},{... | collective-permute-start | bytes 884744 | tf_op jit(solution)/shard_map/ppermute | solution.py:13
  15.8 5.1 %collective-permute-done = bf16[1,6,24,1024]{3,2,1,0:T(8,128)(2,1)S(1)} collective-permute-done((bf16[1,6,24,1024]{3,2,1,0:T(8,128)(2,1)S(1)}, bf16[1,6,24,1024]{3,2,1,0:T(8,128)(2,1)S(1)}, u32[]{:S(2)}, u32[]{:S(2)}) %collective-permute-start) | collective-permute-done | bytes 294944 | tf_op jit(solution)/shard_map/ppermute | solution.py:13
  22.9 2.1 %copy.40 = bf16[128,8,2,512]{3,1,2,0:T(8,128)(2,1)S(1)} copy(bf16[128,8,2,512]{3,2,1,0:T(2,128)(2,1)} %bitcast.102) | data formatting | bytes 4194304
  25.1 9.6 %all-gather.9.cloned.1.call-done = bf16[1024,512]{1,0:T(8,128)(2,1)} async-done(((bf16[512,512]{1,0:T(8,128)(2,1)}), bf16[1024,512]{1,0:T(8,128)(2,1)}) %all-gather.9.cloned.1.call-update) | async-done | bytes 1048592 | tf_op jit(solution)/shard_map/all_gather | solution.py:31
  34.7 2.4 %fusion.12 = bf16[1,12,24,1536]{3,2,1,0:T(8,128)(2,1)S(1)} fusion(bf16[1024,1024]{1,0:T(8,128)(2,1)S(1)} %bitcast.104, bf16[1024,512]{1,0:T(8,128)(2,1)} %all-gather.9.cloned.1.call-done, bf16[6,24,1024]{2,1,0:T(8,128)(2,1)S(1)} %bitcast.106, bf16[6,24,1024]{2,1,0:T(8,128)(2,1)S(1)} %get-tuple-element.28, f32[12,24]{1,0:T(8,128)S(1)} %add_sqrt_fusion.1, ...), kind=kOutput, calls=%fused_computation.17 | convolution fusion | flops 914178048 | bytes 4622592 | tf_op jit(solution)/shard_map/prcd,de->prce/dot_general | solution.py:48
  38.5 3.7 %reshape.311 = bf16[1,12,2,12,3,16,32]{6,5,4,3,2,1,0:T(8,128)(2,1)S(1)} reshape(bf16[1,12,24,1536]{3,2,1,0:T(8,128)(2,1)} %pad_maximum_fusion) | data formatting | bytes 1769472 | tf_op jit(solution)/shard_map/reshape | solution.py:53
  43.4 1.7 copy.39
  47.2 4.0 %fusion.81 = (f32[2,16,144]{2,1,0:T(8,128)S(1)}, f32[2,16,144,144]{2,3,1,0:T(8,128)}) fusion(pred[2,144,144]{1,2,0:T(8,128)(4,1)S(1)} %copy-done.8, bf16[1,2,144,1,16,32]{2,5,4,1,3,0:T(8,128)(2,1)S(1)} %copy-done.7, bf16[1,2,144,1,16,32]{2,5,4,1,3,0:T(8,128)(2,1)S(1)} %copy.38), kind=kOutput, calls=%fused_computation.103 | convolution fusion | flops 45121680 | bytes 3303936 | tf_op jit(solution)/shard_map/sub | solution.py:75
  51.2 2.8 %fusion.23 = bf16[1,2,144,16,32]{2,4,3,1,0:T(8,128)(2,1)S(1)} fusion(f32[2,16,144,144]{2,3,1,0:T(8,128)} %get-tuple-element.33, f32[2,16,144]{2,1,0:T(8,128)S(1)} %get-tuple-element.32, bf16[1,2,144,1,16,32]{2,5,4,1,3,0:T(8,128)(2,1)S(1)} %copy.37), kind=kOutput, calls=%fused_computation.37 | convolution fusion | flops 43941888 | bytes 3262464 | tf_op jit(solution)/shard_map/pnhqk,pnkhd->pnqhd/dot_general | solution.py:77
  56.2 1.8 collective-permute-start.1
  58.0 6.2 %collective-permute-done.1 = bf16[1,6,24,512]{3,2,1,0:T(8,128)(2,1)S(1)} collective-permute-done((bf16[1,6,24,512]{3,2,1,0:T(8,128)(2,1)S(1)}, bf16[1,6,24,512]{3,2,1,0:T(8,128)(2,1)S(1)}, u32[]{:S(2)}, u32[]{:S(2)}) %collective-permute-start.1) | collective-permute-done | bytes 147488 | tf_op jit(solution)/shard_map/ppermute | solution.py:13
  64.1 2.5 %fusion.20 = bf16[1,12,24,1024]{3,2,1,0:T(8,128)(2,1)} fusion(bf16[512,1024]{1,0:T(8,128)(2,1)} %all-gather.13.cloned.1.call-done, bf16[1,12,18,512]{3,2,1,0:T(8,128)(2,1)S(1)} %bitcast.99, bf16[1,12,6,512]{3,2,1,0:T(8,128)(2,1)S(1)} %slice.63, bf16[1,6,24,512]{3,2,1,0:T(8,128)(2,1)S(1)} %collective-permute-done.1), kind=kOutput, calls=%fused_computation.34 | convolution fusion | flops 303169536 | bytes 2080768 | tf_op jit(solution)/shard_map/prce,ed->prcd/dot_general | solution.py:85
  67.5 3.6 %copy.41 = bf16[128,8,2,512]{3,1,2,0:T(8,128)(2,1)} copy(bf16[128,8,2,512]{3,2,1,0:T(2,128)(2,1)} %bitcast.101) | data formatting | bytes 4194304
  71.1 25.1 %all-reduce.2.cloned.1.call-done = bf16[1,12,24,1024]{3,2,1,0:T(8,128)(2,1)} async-done(((bf16[1,12,24,1024]{3,2,1,0:T(8,128)(2,1)}), bf16[1,12,24,1024]{3,2,1,0:T(8,128)(2,1)}) %all-reduce.2.cloned.1.call-update) | async-done | bytes 589840 | tf_op jit(solution)/shard_map/psum | solution.py:88
  101.1 5.6 %all-gather.15.cloned.1.call-done = bf16[1024,512]{1,0:T(8,128)(2,1)} async-done(((bf16[512,512]{1,0:T(8,128)(2,1)}), bf16[1024,512]{1,0:T(8,128)(2,1)}) %all-gather.15.cloned.1.call-update) | async-done | bytes 1048592 | tf_op jit(solution)/shard_map/all_gather | solution.py:34
  109.3 50.8 %all-gather.21.cloned.1.call-done = bf16[1152,1024]{1,0:T(8,128)(2,1)} async-done(((bf16[288,1024]{1,0:T(8,128)(2,1)}), bf16[1152,1024]{1,0:T(8,128)(2,1)}) %all-gather.21.cloned.1.call-update) | async-done | bytes 2359312 | tf_op jit(solution)/shard_map/all_gather | solution.py:115
  160.1 1.8 fusion.79
  162.6 2.5 %multiply_reduce_fusion = (f32[8,256]{1,0:T(8,128)S(1)}, f32[8,256,1152]{2,1,0:T(8,128)S(1)}) fusion(bf16[256,8,64]{0,2,1:T(8,128)(2,1)} %bitcast.108, bf16[1152,8,64]{0,2,1:T(8,128)(2,1)S(1)} %bitcast.97), kind=kOutput, calls=%fused_computation.2 | convolution fusion | flops 306706432 | bytes 10887168 | tf_op jit(solution)/shard_map/while/body/eval_jaxpr/pqhd,pkhd->phqk/dot_general | solution.py:133
  165.1 1.9 fusion.1
  167.0 1.7 copy-done
  169.4 5.5 %fusion.40 = bf16[8,256,64]{1,2,0:T(8,128)(2,1)S(1)} fusion(bf16[1152,8,64]{0,2,1:T(8,128)(2,1)S(1)} %bitcast.105, f32[8,256,1152]{2,1,0:T(8,128)} %copy-done, f32[8,256]{1,0:T(8,128)S(1)} %get-tuple-element.34, f32[8,256]{1,0:T(8,128)S(1)} %get-tuple-element.31, f32[8,256]{1,0:T(8,128)S(1)} %get-tuple-element.30), kind=kOutput, calls=%fused_computation.52 | convolution fusion | flops 309460992 | bytes 10903552 | tf_op jit(solution)/shard_map/while/body/eval_jaxpr/phqk,pkhd->phqd/dot_general | solution.py:140
  175.0 2.5 %fusion.24 = bf16[256,1,1024]{2,0,1:T(8,128)(2,1)} fusion(bf16[256,512]{0,1:T(8,128)(2,1)S(1)} %bitcast.110, bf16[512,1024]{1,0:T(8,128)(2,1)} %all-gather.19.cloned.1.call-done), kind=kOutput, calls=%fused_computation.38 | convolution fusion | flops 268697600 | bytes 1835008 | tf_op jit(solution)/shard_map/pte,ed->tpd/dot_general | solution.py:157
  177.6 13.6 %reduce-scatter.2.cloned.1.call-done = bf16[128,1,1024]{2,0,1:T(8,128)(2,1)} async-done(((bf16[256,1,1024]{2,0,1:T(8,128)(2,1)}), bf16[128,1,1024]{2,0,1:T(8,128)(2,1)}) %reduce-scatter.2.cloned.1.call-update) | async-done | bytes 262160 | tf_op jit(solution)/shard_map/reduce_scatter | solution.py:156
  191.2 1.7 fusion.50
  (80 shorter events, 21.8 us)
Async XLA Ops:
  7.2 2.3 %copy-start.4 = (bf16[1,12,24,1024]{3,2,1,0:T(8,128)(2,1)S(1)}, bf16[1,12,24,1024]{3,2,1,0:T(8,128)(2,1)}, u32[]{:S(2)}) copy-start(bf16[1,12,24,1024]{3,2,1,0:T(8,128)(2,1)} %param.8) | copy-start | bytes 1769476
  7.2 15.8 %all-gather.11.cloned.1.call-start = ((), (), s32[]{:S(2)}) async-start(), calls=%async_computation.2 | async-start | bytes 3145728 | tf_op jit(solution)/shard_map/all_gather | solution.py:32
  7.9 26.8 %all-gather.9.cloned.1.call-start = ((), (), s32[]{:S(2)}) async-start(), calls=%async_computation.1 | async-start | bytes 1572864 | tf_op jit(solution)/shard_map/all_gather | solution.py:31
  8.7 49.3 %all-gather.13.cloned.1.call-start = ((), (), s32[]{:S(2)}) async-start(), calls=%async_computation.3 | async-start | bytes 1572864 | tf_op jit(solution)/shard_map/all_gather | solution.py:33
  9.4 58.1 %all-gather.17.cloned.1.call-start = ((), (), s32[]{:S(2)}) async-start(), calls=%async_computation.6 | async-start | bytes 3145728 | tf_op jit(solution)/shard_map/all_gather | solution.py:35
  9.6 11.4 %collective-permute-start = (bf16[1,6,24,1024]{3,2,1,0:T(8,128)(2,1)S(1)}, bf16[1,6,24,1024]{3,2,1,0:T(8,128)(2,1)S(1)}, u32[]{:S(2)}, u32[]{:S(2)}) collective-permute-start(bf16[1,6,24,1024]{3,2,1,0:T(8,128)(2,1)S(1)} %get-tuple-element.29), channel_id=1, source_target_pairs={{0,12},{4,0},{8,4},{12,8},{1,13},{5,1},{9,5},{13,9},{2,14},{6,2},{... | collective-permute-start | bytes 884744 | tf_op jit(solution)/shard_map/ppermute | solution.py:13
  14.7 81.5 %all-reduce.2.cloned.1.call-start = ((), (), s32[]{:S(2)}) async-start(), calls=%async_computation.4 | async-start | bytes 1179648 | tf_op jit(solution)/shard_map/psum | solution.py:88
  45.1 2.1 %copy-start.7 = (bf16[1,2,144,1,16,32]{2,5,4,1,3,0:T(8,128)(2,1)S(1)}, bf16[1,2,144,1,16,32]{2,5,4,1,3,0:T(8,128)(2,1)}, u32[]{:S(2)}) copy-start(bf16[1,2,144,1,16,32]{2,5,4,1,3,0:T(8,128)(2,1)} %copy.39) | copy-start | bytes 884740
  45.1 2.1 %copy-start.8 = (pred[2,144,144]{1,2,0:T(8,128)(4,1)S(1)}, pred[2,144,144]{1,2,0:T(8,128)(4,1)}, u32[]{:S(2)}) copy-start(pred[2,144,144]{1,2,0:T(8,128)(4,1)} %broadcast_compare_fusion) | copy-start | bytes 124420
  56.2 8.0 %collective-permute-start.1 = (bf16[1,6,24,512]{3,2,1,0:T(8,128)(2,1)S(1)}, bf16[1,6,24,512]{3,2,1,0:T(8,128)(2,1)S(1)}, u32[]{:S(2)}, u32[]{:S(2)}) collective-permute-start(bf16[1,6,24,512]{3,2,1,0:T(8,128)(2,1)S(1)} %fusion.70), channel_id=1, source_target_pairs={{0,4},{4,8},{8,12},{12,0},{1,5},{5,9},{9,13},{13,1},{2,6},{6,10},{... | collective-permute-start | bytes 442376 | tf_op jit(solution)/shard_map/ppermute | solution.py:13
  66.7 40.1 %all-gather.15.cloned.1.call-start = ((), (), s32[]{:S(2)}) async-start(), calls=%async_computation.5 | async-start | bytes 1572864 | tf_op jit(solution)/shard_map/all_gather | solution.py:34
  67.3 92.8 %all-gather.21.cloned.1.call-start = ((), (), s32[]{:S(2)}) async-start(), calls=%async_computation.9 | async-start | bytes 2949120 | tf_op jit(solution)/shard_map/all_gather | solution.py:115
  67.5 28.7 %copy-start.5 = (bf16[1,12,24,1024]{3,2,1,0:T(8,128)(2,1)S(1)}, bf16[1,12,24,1024]{3,2,1,0:T(8,128)(2,1)}, u32[]{:S(2)}) copy-start(bf16[1,12,24,1024]{3,2,1,0:T(8,128)(2,1)} %param.8) | copy-start | bytes 1769476
  96.2 2.0 %copy-start.6 = (bf16[128,8,2,512]{3,1,2,0:T(8,128)(2,1)S(1)}, bf16[128,8,2,512]{3,1,2,0:T(8,128)(2,1)}, u32[]{:S(2)}) copy-start(bf16[128,8,2,512]{3,1,2,0:T(8,128)(2,1)} %copy.41) | copy-start | bytes 6291460
  97.7 2.2 %copy-start.1 = (bf16[1,12,24,1024]{3,2,1,0:T(8,128)(2,1)}, bf16[1,12,24,1024]{3,2,1,0:T(8,128)(2,1)S(1)}, u32[]{:S(2)}) copy-start(bf16[1,12,24,1024]{3,2,1,0:T(8,128)(2,1)S(1)} %get-tuple-element.15) | copy-start | bytes 1769476
  98.2 2.4 %copy-start.2 = (bf16[1,256,1024]{2,1,0:T(8,128)(2,1)S(1)}, bf16[1,256,1024]{2,1,0:T(8,128)(2,1)}, u32[]{:S(2)}) copy-start(bf16[1,256,1024]{2,1,0:T(8,128)(2,1)} %param.9) | copy-start | bytes 1572868
  99.9 75.1 %all-gather.19.cloned.1.call-start = ((), (), s32[]{:S(2)}) async-start(), calls=%async_computation.7 | async-start | bytes 1572864 | tf_op jit(solution)/shard_map/all_gather | solution.py:36
  100.6 90.6 %reduce-scatter.2.cloned.1.call-start = ((), (), s32[]{:S(2)}) async-start(), calls=%async_computation.8 | async-start | bytes 786432 | tf_op jit(solution)/shard_map/reduce_scatter | solution.py:156
  165.1 3.7 %copy-start = (f32[8,256,1152]{2,1,0:T(8,128)}, f32[8,256,1152]{2,1,0:T(8,128)S(1)}, u32[]{:S(2)}) copy-start(f32[8,256,1152]{2,1,0:T(8,128)S(1)} %get-tuple-element.35) | copy-start | bytes 28311556
  175.0 16.3 %copy-start.3 = (bf16[1,256,1024]{2,1,0:T(8,128)(2,1)S(1)}, bf16[1,256,1024]{2,1,0:T(8,128)(2,1)}, u32[]{:S(2)}) copy-start(bf16[1,256,1024]{2,1,0:T(8,128)(2,1)} %param.9) | copy-start | bytes 1572868
Sparse Core Ops, SparseCore 0:
  9.6 13.3 all-gather.10
  24.5 10.1 all-gather.8
  36.3 10.1 all-gather.12
  47.9 11.7 all-gather.16
  66.8 29.3 all-reduce.1
  97.7 9.0 all-gather.14
  108.4 51.6 all-gather.20
  161.7 7.8 all-gather.18
  177.7 13.4 reduce-scatter.1
where the time goes:
time: 200 us; the launch traced here: 199 us
  waiting for transfers between devices  121 us (60%)
  matrix products  25.6 us (13%)
  local copies, waits for them, and re-layouts  22.9 us (11%)
  between operations  14.2 us (7%)
  other arithmetic  8.42 us (4%)
  starting transfers between devices  7.43 us (4%)
    all_gather x1, waiting for transfers between devices, body(): shard_rows = lax.all_gather(page_kv, 'tile', axis=1, tiled=True)  50.8 us
    psum x1, waiting for transfers between devices, body(): lax.psum(partial_proj.astype(jnp.bfloat16), 'mp').astype(jnp.float32)  25.1 us
    reduce_scatter x1, waiting for transfers between devices, body(): lax.psum_scatter(jnp.einsum('pte,ed->tpd', context, wout_dec, preferred_e...  13.6 us
    ppermute x2, waiting for transfers between devices, from_behind(): lax.ppermute(value, axis, [(i, (i + by) % devices) for i in range(devices)])  11.3 us
    unnamed x23, local copies, waits for them, and re-layouts  11.3 us
    all_gather x1, waiting for transfers between devices, body(): lax.all_gather(enc_query, 'batch', axis=0, tiled=True)  9.63 us
    ppermute x2, starting transfers between devices, from_behind(): lax.ppermute(value, axis, [(i, (i + by) % devices) for i in range(devices)])  6.9 us
    all_gather x1, waiting for transfers between devices, body(): lax.all_gather(dec_query, 'batch', axis=0, tiled=True)  5.6 us
  transfers between devices with their start and end apart: 11, of which 8 were waited for; matrix products, arithmetic and copies ran while one was open for 25% of the time, Pallas kernels for 0%

commit v1 on v0

--- a/solution.py
+++ b/solution.py
@@ -85,7 +85,9 @@
     partial_proj = jnp.einsum(
         "prce,ed->prcd", unrolled, wproj_enc, preferred_element_type=jnp.float32
     )
-    summed = lax.psum(partial_proj.astype(jnp.bfloat16), "mp").astype(jnp.float32)
+    summed = jnp.sum(lax.all_gather(partial_proj.astype(jnp.bfloat16), "mp"), axis=0).astype(
+        jnp.float32
+    )
     encoded = (page_cells.astype(jnp.float32) + summed).astype(jnp.bfloat16)
     hq_dec = wq_dec.shape[1]
     heads_dec = hq_dec // HEAD_DEC

time: 200 us -> 193 us (0.965)
  waiting for transfers between devices: 121 us -> 112 us
    psum x1 -> x0, waiting for transfers between devices: 25.1 us -> none  [body(): lax.psum(partial_proj.astype(jnp.bfloat16), 'mp').astype(jnp.float32)]
    all_gather x0 -> x1, waiting for transfers between devices: none -> 17.8 us  [body(): lax.all_gather(partial_proj.astype(jnp.bfloat16), 'mp')]
  transfers between devices with their start and end apart: 11 -> 11, of which waited for: 8 -> 8; matrix products, arithmetic and copies ran while one was open for 25% -> 27% of each run, Pallas kernels for 0% -> 0%
where the time goes in v1:
time: 193 us; the launch traced here: 192 us
  waiting for transfers between devices  112 us (58%)
  matrix products  25.6 us (13%)
  local copies, waits for them, and re-layouts  23.9 us (12%)
  between operations  14.2 us (7%)
  other arithmetic  8.77 us (5%)
  starting transfers between devices  7.43 us (4%)
    all_gather x1, waiting for transfers between devices, body(): shard_rows = lax.all_gather(page_kv, 'tile', axis=1, tiled=True)  50.7 us
    all_gather x1, waiting for transfers between devices, body(): lax.all_gather(partial_proj.astype(jnp.bfloat16), 'mp')  17.8 us
    reduce_scatter x1, waiting for transfers between devices, body(): lax.psum_scatter(jnp.einsum('pte,ed->tpd', context, wout_dec, preferred_e...  13.6 us
    unnamed x23, local copies, waits for them, and re-layouts  12.3 us
    ppermute x2, waiting for transfers between devices, from_behind(): lax.ppermute(value, axis, [(i, (i + by) % devices) for i in range(devices)])  11.3 us
    all_gather x1, waiting for transfers between devices, body(): lax.all_gather(enc_query, 'batch', axis=0, tiled=True)  9.63 us
    ppermute x2, starting transfers between devices, from_behind(): lax.ppermute(value, axis, [(i, (i + by) % devices) for i in range(devices)])  6.9 us
    dot_general x1, matrix products, advance(): jnp.einsum('phqk,pkhd->phqd', expo.astype(jnp.bfloat16), block_vals, pref...  5.51 us
  transfers between devices with their start and end apart: 11, of which 8 were waited for; matrix products, arithmetic and copies ran while one was open for 27% of the time, Pallas kernels for 0%

profile of v1, /device:TPU:0, one launch (start us, length us, event | category | flops | bytes accessed | tf_op | source)
XLA Modules:
  0.0 192.1 jit_solution(4294889195947293891)
XLA Ops:
  9.6 5.1 %collective-permute-start = (bf16[1,6,24,1024]{3,2,1,0:T(8,128)(2,1)S(1)}, bf16[1,6,24,1024]{3,2,1,0:T(8,128)(2,1)S(1)}, u32[]{:S(2)}, u32[]{:S(2)}) collective-permute-start(bf16[1,6,24,1024]{3,2,1,0:T(8,128)(2,1)S(1)} %get-tuple-element.29), channel_id=1, source_target_pairs={{0,12},{4,0},{8,4},{12,8},{1,13},{5,1},{9,5},{13,9},{2,14},{6,2},{... | collective-permute-start | bytes 884744 | tf_op jit(solution)/shard_map/ppermute | solution.py:13
  15.8 5.1 %collective-permute-done = bf16[1,6,24,1024]{3,2,1,0:T(8,128)(2,1)S(1)} collective-permute-done((bf16[1,6,24,1024]{3,2,1,0:T(8,128)(2,1)S(1)}, bf16[1,6,24,1024]{3,2,1,0:T(8,128)(2,1)S(1)}, u32[]{:S(2)}, u32[]{:S(2)}) %collective-permute-start) | collective-permute-done | bytes 294944 | tf_op jit(solution)/shard_map/ppermute | solution.py:13
  22.9 2.1 %copy.40 = bf16[128,8,2,512]{3,1,2,0:T(8,128)(2,1)S(1)} copy(bf16[128,8,2,512]{3,2,1,0:T(2,128)(2,1)} %bitcast.103) | data formatting | bytes 4194304
  25.1 9.6 %all-gather.11.cloned.1.call-done = bf16[1024,512]{1,0:T(8,128)(2,1)} async-done(((bf16[512,512]{1,0:T(8,128)(2,1)}), bf16[1024,512]{1,0:T(8,128)(2,1)}) %all-gather.11.cloned.1.call-update) | async-done | bytes 1048592 | tf_op jit(solution)/shard_map/all_gather | solution.py:31
  34.7 2.4 %fusion.12 = bf16[1,12,24,1536]{3,2,1,0:T(8,128)(2,1)S(1)} fusion(bf16[1024,1024]{1,0:T(8,128)(2,1)S(1)} %bitcast.105, bf16[1024,512]{1,0:T(8,128)(2,1)} %all-gather.11.cloned.1.call-done, bf16[6,24,1024]{2,1,0:T(8,128)(2,1)S(1)} %bitcast.110, bf16[6,24,1024]{2,1,0:T(8,128)(2,1)S(1)} %get-tuple-element.28, f32[12,24]{1,0:T(8,128)S(1)} %add_sqrt_fusion.1, ...), kind=kOutput, calls=%fused_computation.17 | convolution fusion | flops 914178048 | bytes 4622592 | tf_op jit(solution)/shard_map/prcd,de->prce/dot_general | solution.py:48
  38.5 3.7 %reshape.323 = bf16[1,12,2,12,3,16,32]{6,5,4,3,2,1,0:T(8,128)(2,1)S(1)} reshape(bf16[1,12,24,1536]{3,2,1,0:T(8,128)(2,1)} %pad_maximum_fusion) | data formatting | bytes 1769472 | tf_op jit(solution)/shard_map/reshape | solution.py:53
  43.4 1.7 copy.39
  47.2 4.0 %fusion.82 = (f32[2,16,144]{2,1,0:T(8,128)S(1)}, f32[2,16,144,144]{2,3,1,0:T(8,128)}) fusion(pred[2,144,144]{1,2,0:T(8,128)(4,1)S(1)} %copy-done.8, bf16[1,2,144,1,16,32]{2,5,4,1,3,0:T(8,128)(2,1)S(1)} %copy-done.7, bf16[1,2,144,1,16,32]{2,5,4,1,3,0:T(8,128)(2,1)S(1)} %copy.38), kind=kOutput, calls=%fused_computation.103 | convolution fusion | flops 45121680 | bytes 3303936 | tf_op jit(solution)/shard_map/sub | solution.py:75
  51.2 2.8 %fusion.22 = bf16[1,2,144,16,32]{2,4,3,1,0:T(8,128)(2,1)S(1)} fusion(f32[2,16,144,144]{2,3,1,0:T(8,128)} %get-tuple-element.33, f32[2,16,144]{2,1,0:T(8,128)S(1)} %get-tuple-element.32, bf16[1,2,144,1,16,32]{2,5,4,1,3,0:T(8,128)(2,1)S(1)} %copy.37), kind=kOutput, calls=%fused_computation.36 | convolution fusion | flops 43941888 | bytes 3262464 | tf_op jit(solution)/shard_map/pnhqk,pnkhd->pnqhd/dot_general | solution.py:77
  56.2 1.8 collective-permute-start.1
  58.0 6.2 %collective-permute-done.1 = bf16[1,6,24,512]{3,2,1,0:T(8,128)(2,1)S(1)} collective-permute-done((bf16[1,6,24,512]{3,2,1,0:T(8,128)(2,1)S(1)}, bf16[1,6,24,512]{3,2,1,0:T(8,128)(2,1)S(1)}, u32[]{:S(2)}, u32[]{:S(2)}) %collective-permute-start.1) | collective-permute-done | bytes 147488 | tf_op jit(solution)/shard_map/ppermute | solution.py:13
  64.1 2.5 %convolution_convert_fusion.1 = bf16[12,24,1024]{2,1,0:T(8,128)(2,1)} fusion(bf16[512,1024]{1,0:T(8,128)(2,1)} %all-gather.15.cloned.1.call-done, bf16[1,12,18,512]{3,2,1,0:T(8,128)(2,1)S(1)} %bitcast.107, bf16[1,12,6,512]{3,2,1,0:T(8,128)(2,1)S(1)} %slice.63, bf16[1,6,24,512]{3,2,1,0:T(8,128)(2,1)S(1)} %collective-permute-done.1), kind=kOutput, calls=%fused_computation.29 | convolution fusion | flops 303169536 | bytes 2080768 | tf_op jit(solution)/shard_map/prce,ed->prcd/dot_general | solution.py:85
  67.5 3.6 %copy.41 = bf16[128,8,2,512]{3,1,2,0:T(8,128)(2,1)} copy(bf16[128,8,2,512]{3,2,1,0:T(2,128)(2,1)} %bitcast.102) | data formatting | bytes 4194304
  71.1 17.8 %all-gather.23.cloned.1.call-done = bf16[24,24,1024]{2,1,0:T(8,128)(2,1)} async-done(((bf16[12,24,1024]{2,1,0:T(8,128)(2,1)}), bf16[24,24,1024]{2,1,0:T(8,128)(2,1)}) %all-gather.23.cloned.1.call-update) | async-done | bytes 1179664 | tf_op jit(solution)/shard_map/all_gather | solution.py:88
  95.2 4.2 %all-gather.17.cloned.1.call-done = bf16[1024,512]{1,0:T(8,128)(2,1)} async-done(((bf16[512,512]{1,0:T(8,128)(2,1)}), bf16[1024,512]{1,0:T(8,128)(2,1)}) %all-gather.17.cloned.1.call-update) | async-done | bytes 1048592 | tf_op jit(solution)/shard_map/all_gather | solution.py:34
  102.0 50.7 %all-gather.25.cloned.1.call-done = bf16[1152,1024]{1,0:T(8,128)(2,1)} async-done(((bf16[288,1024]{1,0:T(8,128)(2,1)}), bf16[1152,1024]{1,0:T(8,128)(2,1)}) %all-gather.25.cloned.1.call-update) | async-done | bytes 2359312 | tf_op jit(solution)/shard_map/all_gather | solution.py:117
  152.7 1.8 fusion.80
  155.2 2.5 %multiply_reduce_fusion = (f32[8,256]{1,0:T(8,128)S(1)}, f32[8,256,1152]{2,1,0:T(8,128)S(1)}) fusion(bf16[256,8,64]{0,2,1:T(8,128)(2,1)} %bitcast.112, bf16[1152,8,64]{0,2,1:T(8,128)(2,1)S(1)} %bitcast.100), kind=kOutput, calls=%fused_computation.2 | convolution fusion | flops 306706432 | bytes 10887168 | tf_op jit(solution)/shard_map/while/body/eval_jaxpr/pqhd,pkhd->phqk/dot_general | solution.py:135
  157.7 1.9 fusion.1
  159.6 1.7 copy-done
  162.0 5.5 %fusion.40 = bf16[8,256,64]{1,2,0:T(8,128)(2,1)S(1)} fusion(bf16[1152,8,64]{0,2,1:T(8,128)(2,1)S(1)} %bitcast.109, f32[8,256,1152]{2,1,0:T(8,128)} %copy-done, f32[8,256]{1,0:T(8,128)S(1)} %get-tuple-element.34, f32[8,256]{1,0:T(8,128)S(1)} %get-tuple-element.31, f32[8,256]{1,0:T(8,128)S(1)} %get-tuple-element.30), kind=kOutput, calls=%fused_computation.52 | convolution fusion | flops 309460992 | bytes 10903552 | tf_op jit(solution)/shard_map/while/body/eval_jaxpr/phqk,pkhd->phqd/dot_general | solution.py:142
  167.6 2.5 %fusion.23 = bf16[256,1,1024]{2,0,1:T(8,128)(2,1)} fusion(bf16[256,512]{0,1:T(8,128)(2,1)S(1)} %bitcast.114, bf16[512,1024]{1,0:T(8,128)(2,1)} %all-gather.21.cloned.1.call-done), kind=kOutput, calls=%fused_computation.37 | convolution fusion | flops 268697600 | bytes 1835008 | tf_op jit(solution)/shard_map/pte,ed->tpd/dot_general | solution.py:159
  170.2 13.6 %reduce-scatter.2.cloned.1.call-done = bf16[128,1,1024]{2,0,1:T(8,128)(2,1)} async-done(((bf16[256,1,1024]{2,0,1:T(8,128)(2,1)}), bf16[128,1,1024]{2,0,1:T(8,128)(2,1)}) %reduce-scatter.2.cloned.1.call-update) | async-done | bytes 262160 | tf_op jit(solution)/shard_map/reduce_scatter | solution.py:158
  183.8 1.7 fusion.50
  (81 shorter events, 23.1 us)
Async XLA Ops:
  7.2 2.3 %copy-start.4 = (bf16[1,12,24,1024]{3,2,1,0:T(8,128)(2,1)S(1)}, bf16[1,12,24,1024]{3,2,1,0:T(8,128)(2,1)}, u32[]{:S(2)}) copy-start(bf16[1,12,24,1024]{3,2,1,0:T(8,128)(2,1)} %param.8) | copy-start | bytes 1769476
  7.2 15.8 %all-gather.13.cloned.1.call-start = ((), (), s32[]{:S(2)}) async-start(), calls=%async_computation.2 | async-start | bytes 3145728 | tf_op jit(solution)/shard_map/all_gather | solution.py:32
  7.9 26.8 %all-gather.11.cloned.1.call-start = ((), (), s32[]{:S(2)}) async-start(), calls=%async_computation.1 | async-start | bytes 1572864 | tf_op jit(solution)/shard_map/all_gather | solution.py:31
  8.7 49.3 %all-gather.15.cloned.1.call-start = ((), (), s32[]{:S(2)}) async-start(), calls=%async_computation.3 | async-start | bytes 1572864 | tf_op jit(solution)/shard_map/all_gather | solution.py:33
  9.4 58.1 %all-gather.19.cloned.1.call-start = ((), (), s32[]{:S(2)}) async-start(), calls=%async_computation.5 | async-start | bytes 3145728 | tf_op jit(solution)/shard_map/all_gather | solution.py:35
  9.6 11.4 %collective-permute-start = (bf16[1,6,24,1024]{3,2,1,0:T(8,128)(2,1)S(1)}, bf16[1,6,24,1024]{3,2,1,0:T(8,128)(2,1)S(1)}, u32[]{:S(2)}, u32[]{:S(2)}) collective-permute-start(bf16[1,6,24,1024]{3,2,1,0:T(8,128)(2,1)S(1)} %get-tuple-element.29), channel_id=1, source_target_pairs={{0,12},{4,0},{8,4},{12,8},{1,13},{5,1},{9,5},{13,9},{2,14},{6,2},{... | collective-permute-start | bytes 884744 | tf_op jit(solution)/shard_map/ppermute | solution.py:13
  14.7 74.3 %all-gather.23.cloned.1.call-start = ((), (), s32[]{:S(2)}) async-start(), calls=%async_computation.8 | async-start | bytes 1769472 | tf_op jit(solution)/shard_map/all_gather | solution.py:88
  45.1 2.1 %copy-start.7 = (bf16[1,2,144,1,16,32]{2,5,4,1,3,0:T(8,128)(2,1)S(1)}, bf16[1,2,144,1,16,32]{2,5,4,1,3,0:T(8,128)(2,1)}, u32[]{:S(2)}) copy-start(bf16[1,2,144,1,16,32]{2,5,4,1,3,0:T(8,128)(2,1)} %copy.39) | copy-start | bytes 884740
  45.1 2.1 %copy-start.8 = (pred[2,144,144]{1,2,0:T(8,128)(4,1)S(1)}, pred[2,144,144]{1,2,0:T(8,128)(4,1)}, u32[]{:S(2)}) copy-start(pred[2,144,144]{1,2,0:T(8,128)(4,1)} %broadcast_compare_fusion) | copy-start | bytes 124420
  56.2 8.0 %collective-permute-start.1 = (bf16[1,6,24,512]{3,2,1,0:T(8,128)(2,1)S(1)}, bf16[1,6,24,512]{3,2,1,0:T(8,128)(2,1)S(1)}, u32[]{:S(2)}, u32[]{:S(2)}) collective-permute-start(bf16[1,6,24,512]{3,2,1,0:T(8,128)(2,1)S(1)} %fusion.70), channel_id=1, source_target_pairs={{0,4},{4,8},{8,12},{12,0},{1,5},{5,9},{9,13},{13,1},{2,6},{6,10},{... | collective-permute-start | bytes 442376 | tf_op jit(solution)/shard_map/ppermute | solution.py:13
  66.7 32.7 %all-gather.17.cloned.1.call-start = ((), (), s32[]{:S(2)}) async-start(), calls=%async_computation.4 | async-start | bytes 1572864 | tf_op jit(solution)/shard_map/all_gather | solution.py:34
  67.3 85.4 %all-gather.25.cloned.1.call-start = ((), (), s32[]{:S(2)}) async-start(), calls=%async_computation.9 | async-start | bytes 2949120 | tf_op jit(solution)/shard_map/all_gather | solution.py:117
  67.5 23.0 %copy-start.5 = (bf16[1,12,24,1024]{3,2,1,0:T(8,128)(2,1)S(1)}, bf16[1,12,24,1024]{3,2,1,0:T(8,128)(2,1)}, u32[]{:S(2)}) copy-start(bf16[1,12,24,1024]{3,2,1,0:T(8,128)(2,1)} %param.8) | copy-start | bytes 1769476
  90.5 1.8 copy-start.6
  90.8 3.2 %copy-start.1 = (bf16[1,12,24,1024]{3,2,1,0:T(8,128)(2,1)}, bf16[1,12,24,1024]{3,2,1,0:T(8,128)(2,1)S(1)}, u32[]{:S(2)}) copy-start(bf16[1,12,24,1024]{3,2,1,0:T(8,128)(2,1)S(1)} %get-tuple-element.15) | copy-start | bytes 1769476
  92.3 2.4 %copy-start.2 = (bf16[1,256,1024]{2,1,0:T(8,128)(2,1)S(1)}, bf16[1,256,1024]{2,1,0:T(8,128)(2,1)}, u32[]{:S(2)}) copy-start(bf16[1,256,1024]{2,1,0:T(8,128)(2,1)} %param.9) | copy-start | bytes 1572868
  94.0 73.6 %all-gather.21.cloned.1.call-start = ((), (), s32[]{:S(2)}) async-start(), calls=%async_computation.6 | async-start | bytes 1572864 | tf_op jit(solution)/shard_map/all_gather | solution.py:36
  94.7 89.1 %reduce-scatter.2.cloned.1.call-start = ((), (), s32[]{:S(2)}) async-start(), calls=%async_computation.7 | async-start | bytes 786432 | tf_op jit(solution)/shard_map/reduce_scatter | solution.py:158
  157.7 3.7 %copy-start = (f32[8,256,1152]{2,1,0:T(8,128)}, f32[8,256,1152]{2,1,0:T(8,128)S(1)}, u32[]{:S(2)}) copy-start(f32[8,256,1152]{2,1,0:T(8,128)S(1)} %get-tuple-element.35) | copy-start | bytes 28311556
  167.6 16.3 %copy-start.3 = (bf16[1,256,1024]{2,1,0:T(8,128)(2,1)S(1)}, bf16[1,256,1024]{2,1,0:T(8,128)(2,1)}, u32[]{:S(2)}) copy-start(bf16[1,256,1024]{2,1,0:T(8,128)(2,1)} %param.9) | copy-start | bytes 1572868
Sparse Core Ops, SparseCore 0:
  9.6 13.3 all-gather.12
  24.5 10.1 all-gather.10
  36.3 10.1 all-gather.14
  47.9 11.7 all-gather.18
  66.8 22.0 all-gather.22
  90.3 9.0 all-gather.16
  101.0 51.6 all-gather.24
  154.2 7.8 all-gather.20
  170.3 13.4 reduce-scatter.1
